TPU v7x, 128 devices: a whole 4x4x4 slice. The times are simulated.
128 devices in a mesh: gx: 16 (over y_hi, x, core), gy: 8 (over y_lo, z).
Axes of the slice: x: 4, y: 4 (y_hi: 2, y_lo: 2; y = y_hi * 2 + y_lo), z: 4, core: 2. Of those that a mesh axis runs over, the one named last changes fastest.
Arguments:
- res_charge: float32 [262144], P(('gx', 'gy')), may hold values from -6 to 6
- res_frac: float32 [3, 262144], P(None, ('gx', 'gy')), may hold values from 0 to 1
- res_cell: int32 [262144], P(('gx', 'gy')), may hold values from 0 to 65535
- res_count: int32 [128], P(('gx', 'gy')), may hold values from 1024 to 2048, as said below
- mov_charge: float32 [65536], P(('gx', 'gy')), may hold values from -6 to 6
- mov_frac: float32 [3, 65536], P(None, ('gx', 'gy')), may hold values from 0 to 1
- mov_cell: int32 [65536], P(('gx', 'gy')), may hold values from 0 to 65535
- mov_dest: int32 [65536, 1], P(('gx', 'gy')), may hold values from 0 to 127; in each aligned block of 512 rows (0 to 511, 512 to 1023, ...) at most 8 rows name the same one
- fine_taps: float32 [3, 13], replicated, may hold values from -3 to 3
- coarse_taps: float32 [3, 13], replicated, may hold values from -3 to 3
Outputs:
- res_potential: float32 [262144], P(('gx', 'gy'))
- arrived_potential: float32 [128, 1024], P(('gx', 'gy'))
- grid_potential: float32 [512, 128, 128], P('gx', 'gy')
Inputs may be any that keep to these rules, and one draw needn't show every extreme that they name: `res_count`: a multiple of 128; some box has exactly 2048 live atoms. `mov_dest`: among the rows of one source box, at most 8 name the same destination, a bound that some block reaches of them.
All inputs are finite; a program needn't handle non-finite values.
Results may differ from a plain program's by a relative error of at most 0.0048.
Values sent between devices are 32-bit elements; how exact they have to be, the bound alone decides.
A program may use at most 64 MiB of HBM per device.

v0:
```python
import jax
import jax.numpy as jnp
from jax import lax
from jax.sharding import PartitionSpec as P

CX = 32
CY = 16
NZ = 128


def from_behind(value, axis, steps):
    count = lax.axis_size(axis)
    pairs = [(source, (source + steps) % count) for source in range(count)]
    return lax.ppermute(value, axis, pairs)


def padded_2(x, sides, width):
    for axis, dim in sides:
        size, length = (lax.axis_size(axis), x.shape[dim])
        up = [(i, (i + 1) % size) for i in range(size)]
        down = [(j, i) for i, j in up]
        last = lax.slice_in_dim(x, length - width, length, axis=dim)
        initial = lax.slice_in_dim(x, 0, width, axis=dim)
        before = lax.ppermute(last, axis, up)
        after = lax.ppermute(initial, axis, down)
        x = jnp.concatenate([before, x, after], axis=dim)
    return x


def spline_weights(fracs):
    rest = 1.0 - fracs
    cube = fracs * fracs * fracs
    square = fracs * fracs
    return jnp.stack(
        [
            rest * rest * rest / 6.0,
            (3.0 * cube - 6.0 * square + 4.0) / 6.0,
            (-3.0 * cube + 3.0 * square + 3.0 * fracs + 1.0) / 6.0,
            cube / 6.0,
        ]
    )


def stencil(first, weights, length, wrapped):
    columns = jnp.arange(length, dtype=jnp.int32)[None, :]
    result = jnp.zeros((first.shape[0], length), jnp.float32)
    for offset_k in range(4):
        where_at = first + offset_k
        if wrapped:
            where_at = where_at % length
        result = result + jnp.where(columns == where_at[:, None], weights[offset_k][:, None], 0.0)
    return result


def factors(fracs, cells):
    cell_x = cells // (CY * NZ)
    cell_y = cells // NZ % CY
    cell_z = cells % NZ
    x_weights = stencil(cell_x, spline_weights(fracs[0]), CX + 3, False)
    y_weights = stencil(cell_y, spline_weights(fracs[1]), CY + 3, False)
    z_weights = stencil(cell_z, spline_weights(fracs[2]), NZ, True)
    yz_weights = (y_weights[:, :, None] * z_weights[:, None, :]).astype(jnp.bfloat16)
    return (x_weights, yz_weights.reshape(cells.shape[0], (CY + 3) * NZ))


def blocked(charges, fracs, cells):
    rows = charges.shape[0]
    block_rows = min(512, rows)
    blocks = rows // block_rows
    return (
        charges.reshape(blocks, block_rows),
        fracs.reshape(3, blocks, block_rows).transpose(1, 0, 2),
        cells.reshape(blocks, block_rows),
    )


def spread(charges, fracs, cells):

    def advance(running, pieces):
        block_charge, block_frac, block_cell = pieces
        x_weights, yz_weights = factors(block_frac, block_cell)
        x_charge = (x_weights * block_charge[:, None]).astype(jnp.bfloat16)
        added = lax.dot_general(
            x_charge, yz_weights, (((0,), (0,)), ((), ())), preferred_element_type=jnp.float32
        )
        return (running + added, None)

    start_grid = jnp.zeros((CX + 3, (CY + 3) * NZ), jnp.float32)
    running, _ = lax.scan(advance, start_grid, blocked(charges, fracs, cells))
    return running


def sample(half_grid, charges, fracs, cells):

    def evaluate(pieces):
        block_charge, block_frac, block_cell = pieces
        x_weights, yz_weights = factors(block_frac, block_cell)
        partial_value = lax.dot_general(
            half_grid, yz_weights, (((1,), (1,)), ((), ())), preferred_element_type=jnp.float32
        )
        x_plain = lax.optimization_barrier(x_weights.astype(jnp.bfloat16)).astype(jnp.float32)
        return jnp.sum(x_plain.T * partial_value, axis=0)

    return lax.map(evaluate, blocked(charges, fracs, cells)).reshape(-1)


def along(field, filter_taps, along_dim, offset, length):
    summed = jnp.zeros(
        field.shape[:along_dim] + (length,) + field.shape[along_dim + 1 :], jnp.float32
    )
    for tap_index in range(filter_taps.shape[0]):
        summed = summed + filter_taps[tap_index] * lax.slice_in_dim(
            field, offset + tap_index, offset + tap_index + length, axis=along_dim
        )
    return summed


def beside_all(field, filter_taps):
    summed = jnp.zeros_like(field)
    half_width = filter_taps.shape[0] // 2
    for tap_index in range(filter_taps.shape[0]):
        summed = summed + filter_taps[tap_index] * jnp.roll(field, half_width - tap_index, axis=2)
    return summed


def level_field(padded, filter_taps, margin, length_x, length_y):
    half_width = filter_taps.shape[1] // 2
    field = along(padded, filter_taps[0], 0, margin - half_width, length_x)
    field = along(field, filter_taps[1], 1, margin - half_width, length_y)
    return beside_all(field, filter_taps[2])


def coarsen(field):
    size_a, size_b, size_c = field.shape
    return field.reshape(size_a // 2, 2, size_b // 2, 2, size_c // 2, 2).sum(axis=(1, 3, 5))


def on_device(
    res_charge,
    res_frac,
    res_cell,
    res_count,
    mov_charge,
    mov_frac,
    mov_cell,
    mov_dest,
    fine_taps,
    coarse_taps,
):
    count_gx = lax.axis_size("gx")
    count_gy = lax.axis_size("gy")
    devices = count_gx * count_gy
    moving = mov_charge.shape[0]
    slots = 2 * moving // devices
    targets = mov_dest[:, 0]
    hits = (targets[:, None] == jnp.arange(devices, dtype=jnp.int32)[None, :]).astype(jnp.float32)
    positions = jnp.arange(moving, dtype=jnp.int32)
    lower = (positions[:, None] >= positions[None, :]).astype(jnp.float32)
    ranks = jnp.dot(lower, hits, precision=lax.Precision.HIGHEST)
    slot = (jnp.sum(hits * ranks, axis=1) - 1.0).astype(jnp.int32)
    target_slot = targets * slots + slot
    placing = (
        target_slot[:, None] == jnp.arange(devices * slots, dtype=jnp.int32)[None, :]
    ).astype(jnp.float32)
    payload = jnp.concatenate(
        [mov_charge[None, :], mov_frac, (mov_cell.astype(jnp.float32) + 1.0)[None, :]], 0
    )
    packed = jnp.dot(payload, placing, precision=lax.Precision.HIGHEST)
    arrived = lax.all_to_all(
        packed.reshape(5, devices, slots), ("gx", "gy"), split_axis=1, concat_axis=1, tiled=True
    )
    arrived = arrived.reshape(5, devices * slots)
    live = jnp.arange(res_charge.shape[0], dtype=jnp.int32) < res_count[0]
    live_charge = jnp.where(live, res_charge, 0.0)
    resident_grid = spread(live_charge, res_frac, res_cell)
    occupied = arrived[4] > 0.5
    arrived_cell = jnp.maximum(arrived[4] - 1.0, 0.0).astype(jnp.int32)
    arrived_grid = spread(arrived[0], arrived[1:4], arrived_cell)
    extended = (resident_grid + arrived_grid).reshape(CX + 3, CY + 3, NZ)
    upper_x = from_behind(extended[CX:], "gx", 1)
    extended = extended[:CX].at[:3].add(upper_x)
    upper_y = from_behind(extended[:, CY:], "gy", 1)
    charge_grid = extended[:, :CY].at[:, :3].add(upper_y)
    fine_padded = padded_2(charge_grid, (("gx", 0), ("gy", 1)), 9)
    coarse_padded = padded_2(coarsen(charge_grid), (("gx", 0), ("gy", 1)), 8)
    fine_field = level_field(fine_padded, fine_taps, 9, CX + 3, CY + 3)
    coarse_field = level_field(coarse_padded, coarse_taps, 8, CX // 2 + 2, CY // 2 + 2)
    spread_coarse = jnp.repeat(jnp.repeat(jnp.repeat(coarse_field, 2, 0), 2, 1), 2, 2)[
        : CX + 3, : CY + 3
    ]
    field_ext = fine_field + spread_coarse
    grid_potential = field_ext[:CX, :CY]
    half_grid = field_ext.astype(jnp.bfloat16).reshape(CX + 3, (CY + 3) * NZ)
    resident_values = sample(half_grid, live_charge, res_frac, res_cell)
    arrived_values = sample(half_grid, arrived[0], arrived[1:4], arrived_cell)
    res_potential = jnp.where(live, resident_values, 0.0)
    arrived_potential = jnp.where(occupied, arrived_values, 0.0)[None, :]
    return (res_potential, arrived_potential, grid_potential)


def solution(mesh):
    return jax.shard_map(
        on_device,
        mesh=mesh,
        in_specs=(
            P(("gx", "gy")),
            P(None, ("gx", "gy")),
            P(("gx", "gy")),
            P(("gx", "gy")),
            P(("gx", "gy")),
            P(None, ("gx", "gy")),
            P(("gx", "gy")),
            P(("gx", "gy"), None),
            P(),
            P(),
        ),
        out_specs=(P(("gx", "gy")), P(("gx", "gy"), None), P("gx", "gy", None)),
        check_vma=False,
    )
```

profile of v0, /device:TPU:0, one launch (start us, length us, event | category | flops | bytes accessed | tf_op | source)
XLA Modules:
  0.0 182.6 jit_solution(335659025685137201)
XLA Ops:
  3.1 1.5 fusion.156
  5.9 11.7 %all-to-all-start = ((f32[5,128,8]{2,0,1:T(8,128)}), f32[5,128,8]{2,0,1:T(8,128)}, u32[]{:S(2)}, u32[]{:S(2)}) async-start(f32[5,128,8]{2,0,1:T(8,128)} %copy.17), calls=%async_computation | async-start | bytes 1048576 | tf_op jit(solution)/shard_map/all_to_all | solution.py:169
  19.8 9.6 %while.58 = (s32[]{:T(128)}, f32[35,2432]{1,0:T(8,128)S(1)}, s32[4,512]{1,0:T(4,128)S(1)}, f32[4,3,512]{2,1,0:T(4,128)S(1)}, f32[4,512]{1,0:T(4,128)S(1)}, /*index=5*/s32[]{:T(128)}, s32[]{:T(128)}, s32[]{}, s32[]{}) while((s32[]{:T(128)}, f32[35,2432]{1,0:T(8,128)S(1)}, s32[4,512]{1,0:T(4,128)S(1)}, f32[4,3,512]{2,1,0:T(4,128)S(1)}, ...), condition=%wide.region_1.2_spmd.clone, body=%wide.region_0.0_spmd.clone.sunk | while | flops 90961152 | bytes 6397083 | solution.py:89
  20.7 1.5 convolution_add_fusion.4
  23.1 1.5 convolution_add_fusion.4
  25.5 1.5 convolution_add_fusion.4
  34.8 4.8 %while.59 = (s32[]{:T(128)}, f32[35,2432]{1,0:T(8,128)S(1)}, s32[2,512]{1,0:T(2,128)S(1)}, f32[2,3,512]{2,1,0:T(4,128)S(1)}, f32[2,512]{1,0:T(2,128)S(1)}, /*index=5*/s32[]{:T(128)}, s32[]{:T(128)}, s32[]{}, s32[]{}) while((s32[]{:T(128)}, f32[35,2432]{1,0:T(8,128)S(1)}, s32[2,512]{1,0:T(2,128)S(1)}, f32[2,3,512]{2,1,0:T(4,128)S(1)}, ...), condition=%wide.region_4.5_spmd.clone, body=%wide.region_3.4_spmd.clone.sunk | while | flops 90961152 | bytes 6397083 | solution.py:89
  35.7 1.5 convolution_add_fusion.5
  38.1 1.5 convolution_add_fusion.5
  41.8 4.9 %collective-permute-done = f32[3,19,128]{2,1,0:T(8,128)S(1)} collective-permute-done((f32[3,19,128]{2,1,0:T(8,128)S(1)}, f32[3,19,128]{2,1,0:T(8,128)S(1)}, u32[]{:S(2)}, u32[]{:S(2)}) %collective-permute-start) | collective-permute-done | bytes 29216 | tf_op jit(solution)/shard_map/ppermute | solution.py:14
  48.6 4.6 %collective-permute-done.1 = f32[32,3,128]{2,1,0:T(4,128)S(1)} collective-permute-done((f32[32,3,128]{2,1,0:T(4,128)S(1)}, f32[32,3,128]{2,1,0:T(4,128)S(1)}, u32[]{:S(2)}, u32[]{:S(2)}) %collective-permute-start.1) | collective-permute-done | bytes 49184 | tf_op jit(solution)/shard_map/ppermute | solution.py:14
  53.5 18.1 %reshape.3264 = f32[16,2,8,2,64,2]{5,4,3,2,1,0:T(8,128)} reshape(f32[32,16,128]{2,1,0:T(8,128)S(1)} %scatter-add.9) | data formatting | bytes 524288 | tf_op jit(solution)/shard_map/reshape | solution.py:135
  71.6 7.0 %reduce_sum.45 = f32[16,8,64]{2,1,0:T(8,128)S(1)} reduce(f32[16,2,8,2,64,2]{5,4,3,2,1,0:T(8,128)} %reshape.3264, f32[]{:T(128)} %constant.878.clone.1), dimensions={1,3,5}, to_apply=%region_5.6 | reduce | flops 57344 | bytes 294916 | tf_op jit(solution)/shard_map/reduce_sum | solution.py:135
  79.2 5.0 %collective-permute-start.3 = (f32[9,16,128]{2,1,0:T(8,128)S(1)}, f32[9,16,128]{2,1,0:T(8,128)S(1)}, u32[]{:S(2)}, u32[]{:S(2)}) collective-permute-start(f32[9,16,128]{2,1,0:T(8,128)S(1)} %get-tuple-element.678), channel_id=1, source_target_pairs={{8,0},{16,8},{24,16},{32,24},{40,32},{48,40},{56,48},{64,56},{72,6... | collective-permute-start | bytes 221192 | tf_op jit(solution)/shard_map/ppermute | solution.py:25
  84.2 1.5 collective-permute-done.6
  87.9 3.8 %collective-permute-done.2 = f32[9,16,128]{2,1,0:T(8,128)S(1)} collective-permute-done((f32[9,16,128]{2,1,0:T(8,128)S(1)}, f32[9,16,128]{2,1,0:T(8,128)S(1)}, u32[]{:S(2)}, u32[]{:S(2)}) %collective-permute-start.2) | collective-permute-done | bytes 73760 | tf_op jit(solution)/shard_map/ppermute | solution.py:24
  95.3 8.3 %fusion.196 = f32[18,24,64]{2,1,0:T(8,128)S(1)} fusion(f32[32,24,64]{2,1,0:T(8,128)S(1)} %pad_maximum_fusion.2, f32[]{:T(128)} %bitcast.75, f32[]{:T(128)} %bitcast.74, f32[]{:T(128)} %bitcast.73, f32[]{:T(128)} %bitcast.72, f32[]{:T(128)} %bitcast.71, f32[]{:T(128)} %bitcast.70, f32[]{:T(128)} %bitcast.69, f32[]{:T(128)} %bitcast.68, f32[]{:T(128)} %bitcast.67, ...), kind=kLoop, calls=%fused_computation.501 | loop fusion | flops 691200 | bytes 1548340 | tf_op jit(solution)/shard_map/add | solution.py:112
  103.6 8.3 %fusion.208 = f32[18,10,64]{2,1,0:T(8,128)S(1)} fusion(f32[18,24,64]{2,1,0:T(8,128)S(1)} %fusion.196, f32[]{:T(128)} %bitcast.87, f32[]{:T(128)} %bitcast.86, f32[]{:T(128)} %bitcast.85, f32[]{:T(128)} %bitcast.84, f32[]{:T(128)} %bitcast.83, f32[]{:T(128)} %bitcast.82, f32[]{:T(128)} %bitcast.81, f32[]{:T(128)} %bitcast.80, f32[]{:T(128)} %bitcast.79, ...), kind=kLoop, calls=%fused_computation.526 | loop fusion | flops 288000 | bytes 645172 | tf_op jit(solution)/shard_map/add | solution.py:112
  113.2 17.0 %fusion.231 = f32[18,10,64]{2,1,0:T(8,128)S(1)} fusion(f32[18,10,58]{2,1,0:T(8,128)S(1)} %get-tuple-element.680, f32[18,10,6]{2,1,0:T(8,128)S(1)} %get-tuple-element.682, f32[18,10,59]{2,1,0:T(8,128)S(1)} %get-tuple-element.684, f32[18,10,5]{2,1,0:T(8,128)S(1)} %get-tuple-element.686, f32[18,10,60]{2,1,0:T(8,128)S(1)} %get-tuple-element.688, ...), kind=kLoop, calls=%fused_computation.562 | loop fusion | flops 714240 | bytes 1198184 | tf_op jit(solution)/shard_map/add | solution.py:122
  133.0 8.8 %fusion.159 = f32[35,34,128]{2,1,0:T(8,128)S(1)} fusion(f32[50,34,128]{2,1,0:T(8,128)S(1)} %pad_maximum_fusion, f32[]{:T(128)} %bitcast.36, f32[]{:T(128)} %bitcast.35, f32[]{:T(128)} %bitcast.34, f32[]{:T(128)} %bitcast.33, f32[]{:T(128)} %bitcast.32, f32[]{:T(128)} %bitcast.31, f32[]{:T(128)} %bitcast.30, f32[]{:T(128)} %bitcast.29, f32[]{:T(128)} %bitcast.28, ...), kind=kLoop, calls=%fused_computation.422 | loop fusion | flops 3808000 | bytes 8529972 | tf_op jit(solution)/shard_map/add | solution.py:112
  141.7 8.7 %fusion.171 = f32[35,19,128]{2,1,0:T(8,128)S(1)} fusion(f32[35,34,128]{2,1,0:T(8,128)S(1)} %fusion.159, f32[]{:T(128)} %bitcast.48, f32[]{:T(128)} %bitcast.47, f32[]{:T(128)} %bitcast.46, f32[]{:T(128)} %bitcast.45, f32[]{:T(128)} %bitcast.44, f32[]{:T(128)} %bitcast.43, f32[]{:T(128)} %bitcast.42, f32[]{:T(128)} %bitcast.41, f32[]{:T(128)} %bitcast.40, ...), kind=kLoop, calls=%fused_computation.447 | loop fusion | flops 2128000 | bytes 4766772 | tf_op jit(solution)/shard_map/add | solution.py:112
  152.8 18.6 %fusion.241 = (bf16[35,19,128]{2,1,0:T(8,128)(2,1)S(1)}, f32[35,19,128]{2,1,0:T(8,128)S(1)}) fusion(f32[35,19,128]{2,1,0:T(8,128)S(1)} %copy.24, f32[35,19,6]{2,1,0:T(8,128)S(1)} %get-tuple-element.650, f32[35,19,122]{2,1,0:T(8,128)S(1)} %get-tuple-element.652, f32[]{:T(128)} %bitcast.60, f32[35,19,5]{2,1,0:T(8,128)S(1)} %get-tuple-element.654, ...), kind=kLoop, calls=%fused_computation.593 | loop fusion | flops 5447680 | bytes 9363304 | tf_op jit(solution)/shard_map/convert_element_type | solution.py:193
  171.5 6.1 %while.56 = (s32[]{:T(128)}, f32[4,512]{1,0:T(4,128)S(1)}, s32[4,512]{1,0:T(4,128)S(1)}, f32[4,3,512]{2,1,0:T(4,128)S(1)}, bf16[35,2432]{1,0:T(8,128)(2,1)S(1)}, /*index=5*/s32[]{:T(128)}, s32[]{:T(128)}, s32[]{}, s32[]{}) while((s32[]{:T(128)}, f32[4,512]{1,0:T(4,128)S(1)}, s32[4,512]{1,0:T(4,128)S(1)}, f32[4,3,512]{2,1,0:T(4,128)S(1)}, ...), condition=%wide.region_8.9_spmd, body=%wide.region_6.8_spmd.sunk | while | flops 90826240 | bytes 5958033 | solution.py:104
  177.6 3.0 %while.57 = (s32[]{:T(128)}, f32[2,512]{1,0:T(2,128)S(1)}, s32[2,512]{1,0:T(2,128)S(1)}, f32[2,3,512]{2,1,0:T(4,128)S(1)}, bf16[35,2432]{1,0:T(8,128)(2,1)S(1)}, /*index=5*/s32[]{:T(128)}, s32[]{:T(128)}, s32[]{}, s32[]{}) while((s32[]{:T(128)}, f32[2,512]{1,0:T(2,128)S(1)}, s32[2,512]{1,0:T(2,128)S(1)}, f32[2,3,512]{2,1,0:T(4,128)S(1)}, ...), condition=%wide.region_11.12_spmd, body=%wide.region_9.11_spmd.sunk | while | flops 90826240 | bytes 5958033 | solution.py:104
  (257 shorter events, 44.3 us)
Async XLA Ops:
  0.6 16.9 %copy-start = (f32[3,13]{1,0:T(4,128)S(1)}, f32[3,13]{1,0:T(4,128)}, u32[]{:S(2)}) copy-start(f32[3,13]{1,0:T(4,128)} %param.31) | copy-start | bytes 472
  0.6 18.4 %copy-start.3 = (s32[2048]{0:T(1024)S(1)}, s32[2048]{0:T(1024)}, u32[]{:S(2)}) copy-start(s32[2048]{0:T(1024)} %param.24) | copy-start | bytes 24580
  0.7 19.0 %copy-start.4 = (f32[2048]{0:T(1024)S(1)}, f32[2048]{0:T(1024)}, u32[]{:S(2)}) copy-start(f32[2048]{0:T(1024)} %param.22) | copy-start | bytes 24580
  0.7 19.1 %copy-start.2 = (f32[3,2048]{1,0:T(4,128)S(1)}, f32[3,2048]{1,0:T(4,128)}, u32[]{:S(2)}) copy-start(f32[3,2048]{1,0:T(4,128)} %param.23) | copy-start | bytes 73732
  5.9 24.9 %all-to-all-start = ((f32[5,128,8]{2,0,1:T(8,128)}), f32[5,128,8]{2,0,1:T(8,128)}, u32[]{:S(2)}, u32[]{:S(2)}) async-start(f32[5,128,8]{2,0,1:T(8,128)} %copy.17), calls=%async_computation | async-start | bytes 1048576 | tf_op jit(solution)/shard_map/all_to_all | solution.py:169
  19.7 9.6 %copy-start.1 = (f32[3,13]{1,0:T(4,128)S(1)}, f32[3,13]{1,0:T(4,128)}, u32[]{:S(2)}) copy-start(f32[3,13]{1,0:T(4,128)} %param.30) | copy-start | bytes 472
  39.7 7.1 %collective-permute-start = (f32[3,19,128]{2,1,0:T(8,128)S(1)}, f32[3,19,128]{2,1,0:T(8,128)S(1)}, u32[]{:S(2)}, u32[]{:S(2)}) collective-permute-start(f32[3,19,128]{2,1,0:T(8,128)S(1)} %slice.957), channel_id=1, source_target_pairs={{0,8},{8,16},{16,24},{24,32},{32,40},{40,48},{48,56},{56,64},{64,7... | collective-permute-start | bytes 87560 | tf_op jit(solution)/shard_map/ppermute | solution.py:14
  46.8 6.4 %collective-permute-start.1 = (f32[32,3,128]{2,1,0:T(4,128)S(1)}, f32[32,3,128]{2,1,0:T(4,128)S(1)}, u32[]{:S(2)}, u32[]{:S(2)}) collective-permute-start(f32[32,3,128]{2,1,0:T(4,128)S(1)} %slice.1158), channel_id=1, source_target_pairs={{0,1},{1,2},{2,3},{3,4},{4,5},{5,6},{6,7},{7,0},{8,9},{9,10},{10,1... | collective-permute-start | bytes 147464 | tf_op jit(solution)/shard_map/ppermute | solution.py:14
  78.6 5.6 %collective-permute-start.7 = (f32[8,8,64]{2,1,0:T(8,128)S(1)}, f32[8,8,64]{2,1,0:T(8,128)S(1)}, u32[]{:S(2)}, u32[]{:S(2)}) collective-permute-start(f32[8,8,64]{2,1,0:T(8,128)S(1)} %get-tuple-element.704), channel_id=1, source_target_pairs={{8,0},{16,8},{24,16},{32,24},{40,32},{48,40},{56,48},{64,56},{72,6... | collective-permute-start | bytes 49160 | tf_op jit(solution)/shard_map/ppermute | solution.py:25
  78.7 7.0 %collective-permute-start.6 = (f32[8,8,64]{2,1,0:T(8,128)S(1)}, f32[8,8,64]{2,1,0:T(8,128)S(1)}, u32[]{:S(2)}, u32[]{:S(2)}) collective-permute-start(f32[8,8,64]{2,1,0:T(8,128)S(1)} %get-tuple-element.703), channel_id=1, source_target_pairs={{0,8},{8,16},{16,24},{24,32},{32,40},{40,48},{48,56},{56,64},{64,7... | collective-permute-start | bytes 49160 | tf_op jit(solution)/shard_map/ppermute | solution.py:24
  79.2 8.7 %collective-permute-start.3 = (f32[9,16,128]{2,1,0:T(8,128)S(1)}, f32[9,16,128]{2,1,0:T(8,128)S(1)}, u32[]{:S(2)}, u32[]{:S(2)}) collective-permute-start(f32[9,16,128]{2,1,0:T(8,128)S(1)} %get-tuple-element.678), channel_id=1, source_target_pairs={{8,0},{16,8},{24,16},{32,24},{40,32},{48,40},{56,48},{64,56},{72,6... | collective-permute-start | bytes 221192 | tf_op jit(solution)/shard_map/ppermute | solution.py:25
  84.2 7.5 %collective-permute-start.2 = (f32[9,16,128]{2,1,0:T(8,128)S(1)}, f32[9,16,128]{2,1,0:T(8,128)S(1)}, u32[]{:S(2)}, u32[]{:S(2)}) collective-permute-start(f32[9,16,128]{2,1,0:T(8,128)S(1)} %get-tuple-element.677), channel_id=1, source_target_pairs={{0,8},{8,16},{16,24},{24,32},{32,40},{40,48},{48,56},{56,64},{64,7... | collective-permute-start | bytes 221192 | tf_op jit(solution)/shard_map/ppermute | solution.py:24
  85.8 8.1 %collective-permute-start.9 = (f32[32,8,64]{2,1,0:T(8,128)S(1)}, f32[32,8,64]{2,1,0:T(8,128)S(1)}, u32[]{:S(2)}, u32[]{:S(2)}) collective-permute-start(f32[32,8,64]{2,1,0:T(8,128)S(1)} %pad_maximum_fusion.3), channel_id=1, source_target_pairs={{1,0},{2,1},{3,2},{4,3},{5,4},{6,5},{7,6},{0,7},{9,8},{10,9},{11,1... | collective-permute-start | bytes 196616 | tf_op jit(solution)/shard_map/ppermute | solution.py:25
  86.8 8.5 %collective-permute-start.8 = (f32[32,8,64]{2,1,0:T(8,128)S(1)}, f32[32,8,64]{2,1,0:T(8,128)S(1)}, u32[]{:S(2)}, u32[]{:S(2)}) collective-permute-start(f32[32,8,64]{2,1,0:T(8,128)S(1)} %pad_maximum_fusion.3), channel_id=1, source_target_pairs={{0,1},{1,2},{2,3},{3,4},{4,5},{5,6},{6,7},{7,0},{8,9},{9,10},{10,1... | collective-permute-start | bytes 196616 | tf_op jit(solution)/shard_map/ppermute | solution.py:24
  91.8 40.0 %collective-permute-start.5 = (f32[50,9,128]{2,1,0:T(8,128)S(1)}, f32[50,9,128]{2,1,0:T(8,128)S(1)}, u32[]{:S(2)}, u32[]{:S(2)}) collective-permute-start(f32[50,9,128]{2,1,0:T(8,128)S(1)} %get-tuple-element.674), channel_id=1, source_target_pairs={{1,0},{2,1},{3,2},{4,3},{5,4},{6,5},{7,6},{0,7},{9,8},{10,9},{11,1... | collective-permute-start | bytes 691208 | tf_op jit(solution)/shard_map/ppermute | solution.py:25
  92.7 39.1 %collective-permute-start.4 = (f32[50,9,128]{2,1,0:T(8,128)S(1)}, f32[50,9,128]{2,1,0:T(8,128)}, u32[]{:S(2)}, u32[]{:S(2)}) collective-permute-start(f32[50,9,128]{2,1,0:T(8,128)S(1)} %get-tuple-element.673), channel_id=1, source_target_pairs={{0,1},{1,2},{2,3},{3,4},{4,5},{5,6},{6,7},{7,0},{8,9},{9,10},{10,1... | collective-permute-start | bytes 691208 | tf_op jit(solution)/shard_map/ppermute | solution.py:24
where the time goes:
time: 184 us; the launch traced here: 183 us
  other arithmetic  92.7 us (50%)
  local copies, waits for them, and re-layouts  33.2 us (18%)
  starting transfers between devices  21.9 us (12%)
  waiting for transfers between devices  17 us (9%)
  matrix products  14.7 us (8%)
  between operations  1.84 us (1%)
    add x4, other arithmetic, along(): summed + filter_taps[tap_index] * lax.slice_in_dim(field, offset + tap_in...  34 us
    convert_element_type x1, other arithmetic, on_device(): half_grid = field_ext.astype(jnp.bfloat16).reshape(CX + 3, (CY + 3) * NZ)  18.6 us
    reshape x1, local copies, waits for them, and re-layouts, coarsen(): field.reshape(size_a // 2, 2, size_b // 2, 2, size_c // 2, 2)  18.1 us
    add x1, other arithmetic, beside_all(): summed + filter_taps[tap_index] * jnp.roll(field, half_width - tap_index,...  17 us
    all_to_all x1, starting transfers between devices, on_device(): lax.all_to_all(packed.reshape(5, devices, slots), ('gx', 'gy'), split_axi...  11.7 us
    ppermute x2, waiting for transfers between devices, from_behind(): return lax.ppermute(value, axis, pairs)  9.57 us
    dot_general x6, matrix products, advance(): lax.dot_general(x_charge, yz_weights, (((0,), (0,)), ((), ())), preferred...  8.92 us
    convert_element_type x12, other arithmetic, factors(): (y_weights[:, :, None] * z_weights[:, None, :]).astype(jnp.bfloat16)  7.11 us
  transfers between devices with their start and end apart: 11, of which 6 were waited for; matrix products, arithmetic and copies ran while one was open for 28% of the time, Pallas kernels for 0%

commit v1 on v0

--- a/solution.py
+++ b/solution.py
@@ -166,8 +166,16 @@
         [mov_charge[None, :], mov_frac, (mov_cell.astype(jnp.float32) + 1.0)[None, :]], 0
     )
     packed = jnp.dot(payload, placing, precision=lax.Precision.HIGHEST)
-    arrived = lax.all_to_all(
-        packed.reshape(5, devices, slots), ("gx", "gy"), split_axis=1, concat_axis=1, tiled=True
+    arrived = jnp.concatenate(
+        lax.all_to_all(
+            jnp.stack(
+                jnp.split(packed.reshape(5, devices, slots), lax.axis_size(("gx", "gy")), axis=1)
+            ),
+            ("gx", "gy"),
+            0,
+            0,
+        ),
+        axis=1,
     )
     arrived = arrived.reshape(5, devices * slots)
     live = jnp.arange(res_charge.shape[0], dtype=jnp.int32) < res_count[0]

time: 184 us -> 185 us (level)
    another operation x1 -> x10, local copies, waits for them, and re-layouts: 0.02 us -> 2.05 us  [the longest x9 2.04 us: on_device(): jnp.stack(jnp.split(packed.reshape(5, devices, slots), lax.axis_size(('gx...]
  transfers between devices with their start and end apart: 11 -> 11, of which waited for: 6 -> 5; matrix products, arithmetic and copies ran while one was open for 28% -> 28% of each run, Pallas kernels for 0% -> 0%
where the time goes in v1:
time: 185 us; the launch traced here: 184 us
  other arithmetic  92.6 us (50%)
  local copies, waits for them, and re-layouts  34 us (18%)
  starting transfers between devices  23 us (12%)
  waiting for transfers between devices  16.2 us (9%)
  matrix products  14.7 us (8%)
  between operations  1.91 us (1%)
    add x4, other arithmetic, along(): summed + filter_taps[tap_index] * lax.slice_in_dim(field, offset + tap_in...  34.1 us
    convert_element_type x1, other arithmetic, on_device(): half_grid = field_ext.astype(jnp.bfloat16).reshape(CX + 3, (CY + 3) * NZ)  18.8 us
    reshape x1, local copies, waits for them, and re-layouts, coarsen(): field.reshape(size_a // 2, 2, size_b // 2, 2, size_c // 2, 2)  18.1 us
    add x1, other arithmetic, beside_all(): summed + filter_taps[tap_index] * jnp.roll(field, half_width - tap_index,...  17 us
    all_to_all x1, starting transfers between devices, on_device(): lax.all_to_all(jnp.stack(jnp.split(packed.reshape(5, devices, slots), lax...  11.6 us
    ppermute x2, waiting for transfers between devices, from_behind(): return lax.ppermute(value, axis, pairs)  9.04 us
    dot_general x6, matrix products, advance(): lax.dot_general(x_charge, yz_weights, (((0,), (0,)), ((), ())), preferred...  8.92 us
    ppermute x4, starting transfers between devices, padded_2(): after = lax.ppermute(initial, axis, down)  8.63 us
  transfers between devices with their start and end apart: 11, of which 5 were waited for; matrix products, arithmetic and copies ran while one was open for 28% of the time, Pallas kernels for 0%

profile of v1, /device:TPU:0, one launch (start us, length us, event | category | flops | bytes accessed | tf_op | source)
XLA Modules:
  0.0 183.6 jit_solution(15289435947785960863)
XLA Ops:
  3.1 1.5 fusion.156
  6.9 11.6 %all-to-all-start = ((f32[128,5,1,8]{3,2,1,0:T(1,128)}), f32[128,5,1,8]{3,2,1,0:T(1,128)}, u32[]{:S(2)}, u32[]{:S(2)}) async-start(f32[128,5,1,8]{3,2,1,0:T(1,128)} %copy.288), calls=%async_computation | async-start | bytes 655360 | tf_op jit(solution)/shard_map/all_to_all | solution.py:170
  20.8 9.6 %while.58 = (s32[]{:T(128)}, f32[35,2432]{1,0:T(8,128)S(1)}, s32[4,512]{1,0:T(4,128)S(1)}, f32[4,3,512]{2,1,0:T(4,128)S(1)}, f32[4,512]{1,0:T(4,128)S(1)}, /*index=5*/s32[]{:T(128)}, s32[]{:T(128)}, s32[]{}, s32[]{}) while((s32[]{:T(128)}, f32[35,2432]{1,0:T(8,128)S(1)}, s32[4,512]{1,0:T(4,128)S(1)}, f32[4,3,512]{2,1,0:T(4,128)S(1)}, ...), condition=%wide.region_1.2_spmd.clone, body=%wide.region_0.0_spmd.clone.sunk | while | flops 90961152 | bytes 6397083 | solution.py:89
  21.7 1.5 convolution_add_fusion.4
  24.1 1.5 convolution_add_fusion.4
  34.6 4.8 %while.59 = (s32[]{:T(128)}, f32[35,2432]{1,0:T(8,128)S(1)}, s32[2,512]{1,0:T(2,128)S(1)}, f32[2,3,512]{2,1,0:T(4,128)S(1)}, f32[2,512]{1,0:T(2,128)S(1)}, /*index=5*/s32[]{:T(128)}, s32[]{:T(128)}, s32[]{}, s32[]{}) while((s32[]{:T(128)}, f32[35,2432]{1,0:T(8,128)S(1)}, s32[2,512]{1,0:T(2,128)S(1)}, f32[2,3,512]{2,1,0:T(4,128)S(1)}, ...), condition=%wide.region_4.5_spmd.clone, body=%wide.region_3.4_spmd.clone.sunk | while | flops 90961152 | bytes 6397083 | solution.py:89
  35.5 1.5 convolution_add_fusion.5
  37.9 1.5 convolution_add_fusion.5
  41.7 4.9 %collective-permute-done = f32[3,19,128]{2,1,0:T(8,128)S(1)} collective-permute-done((f32[3,19,128]{2,1,0:T(8,128)S(1)}, f32[3,19,128]{2,1,0:T(8,128)S(1)}, u32[]{:S(2)}, u32[]{:S(2)}) %collective-permute-start) | collective-permute-done | bytes 29216 | tf_op jit(solution)/shard_map/ppermute | solution.py:14
  48.9 4.2 %collective-permute-done.1 = f32[32,3,128]{2,1,0:T(4,128)S(1)} collective-permute-done((f32[32,3,128]{2,1,0:T(4,128)S(1)}, f32[32,3,128]{2,1,0:T(4,128)S(1)}, u32[]{:S(2)}, u32[]{:S(2)}) %collective-permute-start.1) | collective-permute-done | bytes 49184 | tf_op jit(solution)/shard_map/ppermute | solution.py:14
  53.3 18.1 %reshape.3267 = f32[16,2,8,2,64,2]{5,4,3,2,1,0:T(8,128)} reshape(f32[32,16,128]{2,1,0:T(8,128)S(1)} %scatter-add.9) | data formatting | bytes 524288 | tf_op jit(solution)/shard_map/reshape | solution.py:135
  71.4 7.0 %reduce_sum.45 = f32[16,8,64]{2,1,0:T(8,128)S(1)} reduce(f32[16,2,8,2,64,2]{5,4,3,2,1,0:T(8,128)} %reshape.3267, f32[]{:T(128)} %constant.878.clone.1), dimensions={1,3,5}, to_apply=%region_5.6 | reduce | flops 57344 | bytes 294916 | tf_op jit(solution)/shard_map/reduce_sum | solution.py:135
  79.2 5.3 %collective-permute-start.3 = (f32[9,16,128]{2,1,0:T(8,128)S(1)}, f32[9,16,128]{2,1,0:T(8,128)S(1)}, u32[]{:S(2)}, u32[]{:S(2)}) collective-permute-start(f32[9,16,128]{2,1,0:T(8,128)S(1)} %get-tuple-element.826), channel_id=1, source_target_pairs={{8,0},{16,8},{24,16},{32,24},{40,32},{48,40},{56,48},{64,56},{72,6... | collective-permute-start | bytes 221192 | tf_op jit(solution)/shard_map/ppermute | solution.py:25
  84.5 1.5 collective-permute-done.6
  88.1 3.9 %collective-permute-done.2 = f32[9,16,128]{2,1,0:T(8,128)S(1)} collective-permute-done((f32[9,16,128]{2,1,0:T(8,128)S(1)}, f32[9,16,128]{2,1,0:T(8,128)S(1)}, u32[]{:S(2)}, u32[]{:S(2)}) %collective-permute-start.2) | collective-permute-done | bytes 73760 | tf_op jit(solution)/shard_map/ppermute | solution.py:24
  94.2 1.8 collective-permute-done.8
  96.0 8.3 %fusion.196 = f32[18,24,64]{2,1,0:T(8,128)S(1)} fusion(f32[32,24,64]{2,1,0:T(8,128)S(1)} %pad_maximum_fusion.2, f32[]{:T(128)} %bitcast.204, f32[]{:T(128)} %bitcast.203, f32[]{:T(128)} %bitcast.202, f32[]{:T(128)} %bitcast.201, f32[]{:T(128)} %bitcast.200, f32[]{:T(128)} %bitcast.199, f32[]{:T(128)} %bitcast.198, f32[]{:T(128)} %bitcast.197, f32[]{:T(128)} %bitcast.196, ...), kind=kLoop, calls=%fused_computation.501 | loop fusion | flops 691200 | bytes 1548340 | tf_op jit(solution)/shard_map/add | solution.py:112
  104.3 8.2 %fusion.208 = f32[18,10,64]{2,1,0:T(8,128)S(1)} fusion(f32[18,24,64]{2,1,0:T(8,128)S(1)} %fusion.196, f32[]{:T(128)} %bitcast.216, f32[]{:T(128)} %bitcast.215, f32[]{:T(128)} %bitcast.214, f32[]{:T(128)} %bitcast.213, f32[]{:T(128)} %bitcast.212, f32[]{:T(128)} %bitcast.211, f32[]{:T(128)} %bitcast.210, f32[]{:T(128)} %bitcast.209, f32[]{:T(128)} %bitcast.208, ...), kind=kLoop, calls=%fused_computation.526 | loop fusion | flops 288000 | bytes 645172 | tf_op jit(solution)/shard_map/add | solution.py:112
  113.8 17.0 %fusion.231 = f32[18,10,64]{2,1,0:T(8,128)S(1)} fusion(f32[18,10,58]{2,1,0:T(8,128)S(1)} %get-tuple-element.828, f32[18,10,6]{2,1,0:T(8,128)S(1)} %get-tuple-element.830, f32[18,10,59]{2,1,0:T(8,128)S(1)} %get-tuple-element.832, f32[18,10,5]{2,1,0:T(8,128)S(1)} %get-tuple-element.834, f32[18,10,60]{2,1,0:T(8,128)S(1)} %get-tuple-element.836, ...), kind=kLoop, calls=%fused_computation.562 | loop fusion | flops 714240 | bytes 1198184 | tf_op jit(solution)/shard_map/add | solution.py:122
  133.6 8.8 %fusion.159 = f32[35,34,128]{2,1,0:T(8,128)S(1)} fusion(f32[50,34,128]{2,1,0:T(8,128)S(1)} %pad_maximum_fusion, f32[]{:T(128)} %bitcast.165, f32[]{:T(128)} %bitcast.164, f32[]{:T(128)} %bitcast.163, f32[]{:T(128)} %bitcast.162, f32[]{:T(128)} %bitcast.161, f32[]{:T(128)} %bitcast.160, f32[]{:T(128)} %bitcast.159, f32[]{:T(128)} %bitcast.158, f32[]{:T(128)} %bitcast.157, ...), kind=kLoop, calls=%fused_computation.422 | loop fusion | flops 3808000 | bytes 8529972 | tf_op jit(solution)/shard_map/add | solution.py:112
  142.4 8.9 %fusion.171 = f32[35,19,128]{2,1,0:T(8,128)S(1)} fusion(f32[35,34,128]{2,1,0:T(8,128)S(1)} %fusion.159, f32[]{:T(128)} %bitcast.177, f32[]{:T(128)} %bitcast.176, f32[]{:T(128)} %bitcast.175, f32[]{:T(128)} %bitcast.174, f32[]{:T(128)} %bitcast.173, f32[]{:T(128)} %bitcast.172, f32[]{:T(128)} %bitcast.171, f32[]{:T(128)} %bitcast.170, f32[]{:T(128)} %bitcast.169, ...), kind=kLoop, calls=%fused_computation.447 | loop fusion | flops 2128000 | bytes 4766772 | tf_op jit(solution)/shard_map/add | solution.py:112
  153.7 18.8 %fusion.241 = (bf16[35,19,128]{2,1,0:T(8,128)(2,1)S(1)}, f32[35,19,128]{2,1,0:T(8,128)S(1)}) fusion(f32[35,19,128]{2,1,0:T(8,128)S(1)} %copy.295, f32[35,19,6]{2,1,0:T(8,128)S(1)} %get-tuple-element.670, f32[35,19,122]{2,1,0:T(8,128)S(1)} %get-tuple-element.672, f32[]{:T(128)} %bitcast.189, f32[35,19,5]{2,1,0:T(8,128)S(1)} %get-tuple-element.674, ...), kind=kLoop, calls=%fused_computation.721 | loop fusion | flops 5447680 | bytes 9363304 | tf_op jit(solution)/shard_map/convert_element_type | solution.py:201
  172.5 6.1 %while.56 = (s32[]{:T(128)}, f32[4,512]{1,0:T(4,128)S(1)}, s32[4,512]{1,0:T(4,128)S(1)}, f32[4,3,512]{2,1,0:T(4,128)S(1)}, bf16[35,2432]{1,0:T(8,128)(2,1)S(1)}, /*index=5*/s32[]{:T(128)}, s32[]{:T(128)}, s32[]{}, s32[]{}) while((s32[]{:T(128)}, f32[4,512]{1,0:T(4,128)S(1)}, s32[4,512]{1,0:T(4,128)S(1)}, f32[4,3,512]{2,1,0:T(4,128)S(1)}, ...), condition=%wide.region_8.9_spmd, body=%wide.region_6.8_spmd.sunk | while | flops 90826240 | bytes 5958033 | solution.py:104
  178.6 3.0 %while.57 = (s32[]{:T(128)}, f32[2,512]{1,0:T(2,128)S(1)}, s32[2,512]{1,0:T(2,128)S(1)}, f32[2,3,512]{2,1,0:T(4,128)S(1)}, bf16[35,2432]{1,0:T(8,128)(2,1)S(1)}, /*index=5*/s32[]{:T(128)}, s32[]{:T(128)}, s32[]{}, s32[]{}) while((s32[]{:T(128)}, f32[2,512]{1,0:T(2,128)S(1)}, s32[2,512]{1,0:T(2,128)S(1)}, f32[2,3,512]{2,1,0:T(4,128)S(1)}, ...), condition=%wide.region_11.12_spmd, body=%wide.region_9.11_spmd.sunk | while | flops 90826240 | bytes 5958033 | solution.py:104
  (265 shorter events, 44.9 us)
Async XLA Ops:
  0.6 17.9 %copy-start = (f32[3,13]{1,0:T(4,128)S(1)}, f32[3,13]{1,0:T(4,128)}, u32[]{:S(2)}) copy-start(f32[3,13]{1,0:T(4,128)} %param.31) | copy-start | bytes 472
  0.6 19.4 %copy-start.3 = (s32[2048]{0:T(1024)S(1)}, s32[2048]{0:T(1024)}, u32[]{:S(2)}) copy-start(s32[2048]{0:T(1024)} %param.24) | copy-start | bytes 24580
  0.7 20.1 %copy-start.4 = (f32[2048]{0:T(1024)S(1)}, f32[2048]{0:T(1024)}, u32[]{:S(2)}) copy-start(f32[2048]{0:T(1024)} %param.22) | copy-start | bytes 24580
  0.7 20.1 %copy-start.2 = (f32[3,2048]{1,0:T(4,128)S(1)}, f32[3,2048]{1,0:T(4,128)}, u32[]{:S(2)}) copy-start(f32[3,2048]{1,0:T(4,128)} %param.23) | copy-start | bytes 73732
  6.9 24.2 %all-to-all-start = ((f32[128,5,1,8]{3,2,1,0:T(1,128)}), f32[128,5,1,8]{3,2,1,0:T(1,128)}, u32[]{:S(2)}, u32[]{:S(2)}) async-start(f32[128,5,1,8]{3,2,1,0:T(1,128)} %copy.288), calls=%async_computation | async-start | bytes 655360 | tf_op jit(solution)/shard_map/all_to_all | solution.py:170
  20.8 9.6 %copy-start.1 = (f32[3,13]{1,0:T(4,128)S(1)}, f32[3,13]{1,0:T(4,128)}, u32[]{:S(2)}) copy-start(f32[3,13]{1,0:T(4,128)} %param.30) | copy-start | bytes 472
  39.5 7.1 %collective-permute-start = (f32[3,19,128]{2,1,0:T(8,128)S(1)}, f32[3,19,128]{2,1,0:T(8,128)S(1)}, u32[]{:S(2)}, u32[]{:S(2)}) collective-permute-start(f32[3,19,128]{2,1,0:T(8,128)S(1)} %slice.957), channel_id=1, source_target_pairs={{0,8},{8,16},{16,24},{24,32},{32,40},{40,48},{48,56},{56,64},{64,7... | collective-permute-start | bytes 87560 | tf_op jit(solution)/shard_map/ppermute | solution.py:14
  46.6 6.4 %collective-permute-start.1 = (f32[32,3,128]{2,1,0:T(4,128)S(1)}, f32[32,3,128]{2,1,0:T(4,128)S(1)}, u32[]{:S(2)}, u32[]{:S(2)}) collective-permute-start(f32[32,3,128]{2,1,0:T(4,128)S(1)} %slice.1158), channel_id=1, source_target_pairs={{0,1},{1,2},{2,3},{3,4},{4,5},{5,6},{6,7},{7,0},{8,9},{9,10},{10,1... | collective-permute-start | bytes 147464 | tf_op jit(solution)/shard_map/ppermute | solution.py:14
  78.4 6.1 %collective-permute-start.7 = (f32[8,8,64]{2,1,0:T(8,128)S(1)}, f32[8,8,64]{2,1,0:T(8,128)S(1)}, u32[]{:S(2)}, u32[]{:S(2)}) collective-permute-start(f32[8,8,64]{2,1,0:T(8,128)S(1)} %get-tuple-element.852), channel_id=1, source_target_pairs={{8,0},{16,8},{24,16},{32,24},{40,32},{48,40},{56,48},{64,56},{72,6... | collective-permute-start | bytes 49160 | tf_op jit(solution)/shard_map/ppermute | solution.py:25
  79.0 7.0 %collective-permute-start.6 = (f32[8,8,64]{2,1,0:T(8,128)S(1)}, f32[8,8,64]{2,1,0:T(8,128)S(1)}, u32[]{:S(2)}, u32[]{:S(2)}) collective-permute-start(f32[8,8,64]{2,1,0:T(8,128)S(1)} %get-tuple-element.851), channel_id=1, source_target_pairs={{0,8},{8,16},{16,24},{24,32},{32,40},{40,48},{48,56},{56,64},{64,7... | collective-permute-start | bytes 49160 | tf_op jit(solution)/shard_map/ppermute | solution.py:24
  79.2 8.9 %collective-permute-start.3 = (f32[9,16,128]{2,1,0:T(8,128)S(1)}, f32[9,16,128]{2,1,0:T(8,128)S(1)}, u32[]{:S(2)}, u32[]{:S(2)}) collective-permute-start(f32[9,16,128]{2,1,0:T(8,128)S(1)} %get-tuple-element.826), channel_id=1, source_target_pairs={{8,0},{16,8},{24,16},{32,24},{40,32},{48,40},{56,48},{64,56},{72,6... | collective-permute-start | bytes 221192 | tf_op jit(solution)/shard_map/ppermute | solution.py:25
  84.5 7.5 %collective-permute-start.2 = (f32[9,16,128]{2,1,0:T(8,128)S(1)}, f32[9,16,128]{2,1,0:T(8,128)S(1)}, u32[]{:S(2)}, u32[]{:S(2)}) collective-permute-start(f32[9,16,128]{2,1,0:T(8,128)S(1)} %get-tuple-element.825), channel_id=1, source_target_pairs={{0,8},{8,16},{16,24},{24,32},{32,40},{40,48},{48,56},{56,64},{64,7... | collective-permute-start | bytes 221192 | tf_op jit(solution)/shard_map/ppermute | solution.py:24
  86.0 8.2 %collective-permute-start.9 = (f32[32,8,64]{2,1,0:T(8,128)S(1)}, f32[32,8,64]{2,1,0:T(8,128)S(1)}, u32[]{:S(2)}, u32[]{:S(2)}) collective-permute-start(f32[32,8,64]{2,1,0:T(8,128)S(1)} %pad_maximum_fusion.3), channel_id=1, source_target_pairs={{1,0},{2,1},{3,2},{4,3},{5,4},{6,5},{7,6},{0,7},{9,8},{10,9},{11,1... | collective-permute-start | bytes 196616 | tf_op jit(solution)/shard_map/ppermute | solution.py:25
  87.4 8.5 %collective-permute-start.8 = (f32[32,8,64]{2,1,0:T(8,128)S(1)}, f32[32,8,64]{2,1,0:T(8,128)S(1)}, u32[]{:S(2)}, u32[]{:S(2)}) collective-permute-start(f32[32,8,64]{2,1,0:T(8,128)S(1)} %pad_maximum_fusion.3), channel_id=1, source_target_pairs={{0,1},{1,2},{2,3},{3,4},{4,5},{5,6},{6,7},{7,0},{8,9},{9,10},{10,1... | collective-permute-start | bytes 196616 | tf_op jit(solution)/shard_map/ppermute | solution.py:24
  92.1 40.4 %collective-permute-start.5 = (f32[50,9,128]{2,1,0:T(8,128)S(1)}, f32[50,9,128]{2,1,0:T(8,128)S(1)}, u32[]{:S(2)}, u32[]{:S(2)}) collective-permute-start(f32[50,9,128]{2,1,0:T(8,128)S(1)} %get-tuple-element.694), channel_id=1, source_target_pairs={{1,0},{2,1},{3,2},{4,3},{5,4},{6,5},{7,6},{0,7},{9,8},{10,9},{11,1... | collective-permute-start | bytes 691208 | tf_op jit(solution)/shard_map/ppermute | solution.py:25
  93.4 39.1 %collective-permute-start.4 = (f32[50,9,128]{2,1,0:T(8,128)S(1)}, f32[50,9,128]{2,1,0:T(8,128)}, u32[]{:S(2)}, u32[]{:S(2)}) collective-permute-start(f32[50,9,128]{2,1,0:T(8,128)S(1)} %get-tuple-element.693), channel_id=1, source_target_pairs={{0,1},{1,2},{2,3},{3,4},{4,5},{5,6},{6,7},{7,0},{8,9},{9,10},{10,1... | collective-permute-start | bytes 691208 | tf_op jit(solution)/shard_map/ppermute | solution.py:24
